TPU v7x, 256 devices: a whole 4x4x8 slice. The times are simulated.
256 devices in a mesh: gx: 16 (over x, y), gy: 2 (over core), gz: 8 (over z).
Axes of the slice: x: 4, y: 4, z: 8, core: 2. Of those that a mesh axis runs over, the one named last changes fastest.
Arguments:
- field: float32 [2, 1024, 128, 1024], P(None, 'gx', 'gy', 'gz'), as said below
- start_basis: float32 [1024, 256], replicated, may hold values from -6 to 6
Outputs:
- factor: float32 [1024, 256], P('gx')
- core: float32 [2, 256, 128, 1024], P(None, 'gx', 'gy', 'gz')
Inputs may be any that keep to these rules, and one draw needn't show every extreme that they name: Real-valued field; no structure is promised.
All inputs are finite; a program needn't handle non-finite values.
Results may differ from a plain program's by a relative error of at most 0.0002.
Values sent between devices are 32-bit elements; how exact they have to be, the bound alone decides.
A program may use at most 64 MiB of HBM per device.

v0:
```python
import jax
import jax.numpy as jnp
from jax import lax
from jax.sharding import PartitionSpec as P

ITERS = 2


def orthonormal(image):
    small = jnp.dot(image.T, image, precision=lax.Precision.HIGHEST)
    lower = jnp.linalg.cholesky(small)
    return jax.scipy.linalg.solve_triangular(lower, image.T, lower=True).T


def per_device(field, start_basis):
    comps, slab, cells_y, cells_z = field.shape
    flat_field = field.reshape(comps, slab, cells_y * cells_z)
    fibers = lax.all_to_all(flat_field, "gx", split_axis=2, concat_axis=1, tiled=True)
    basis = start_basis
    local_gram = jnp.einsum("crm,csm->rs", fibers, fibers, precision=lax.Precision.HIGHEST)
    gram = lax.psum(local_gram, ("gx", "gy", "gz"))
    for step in range(ITERS):
        image = jnp.dot(gram, basis, precision=lax.Precision.HIGHEST)
        basis = orthonormal(image)
    projected = jnp.einsum("rk,crm->ckm", basis, fibers, precision=lax.Precision.HIGHEST)
    returned = lax.all_to_all(projected, "gx", split_axis=1, concat_axis=2, tiled=True)
    offset = lax.axis_index("gx") * slab
    factor = lax.dynamic_slice_in_dim(basis, offset, slab, 0)
    return (factor, returned.reshape(comps, returned.shape[1], cells_y, cells_z))


def solution(mesh):
    placed = (P(None, "gx", "gy", "gz"), P())
    return jax.shard_map(
        per_device,
        mesh=mesh,
        in_specs=placed,
        out_specs=(P("gx", None), P(None, "gx", "gy", "gz")),
        check_vma=False,
    )
```

profile of v0, /device:TPU:97, one launch (start us, length us, event | category | flops | bytes accessed | tf_op | source)
XLA Modules:
  0.0 604.0 jit_solution(12621777568615691695)
XLA Ops:
  7.2 8.4 %copy.13 = f32[2,64,64,128]{1,0,3,2:T(2,128)} copy(f32[2,64,64,128]{3,2,1,0:T(8,128)} %param.5) | data formatting | bytes 8388608 | tf_op args[0]
  15.7 15.1 %reshape.52 = f32[16,1,65536]{2,1,0:T(1,128)} reshape(f32[8192,2,64]{2,1,0:T(2,128)} %bitcast.97) | data formatting | bytes 8388608
  30.8 56.1 %all_to_all.33 = f32[16,1,65536]{2,1,0:T(1,128)} all-to-all(f32[16,1,65536]{2,1,0:T(1,128)} %reshape.52), channel_id=1, replica_groups=mesh['gx'=16,'gy'=2,'gz'=8] {'gx'}, dimensions={0} | all-to-all | bytes 8388608 | tf_op jit(solution)/shard_map/all_to_all | solution.py:18
  87.3 13.7 %reduce.8 = f32[16,65536]{1,0:T(8,128)} reduce(f32[16,1,65536]{2,1,0:T(1,128)} %all_to_all.33, f32[]{:T(128)} %broadcast.87), dimensions={1}, to_apply=%all_to_all.24.reduce_sub_computation | reduce | bytes 8388612 | tf_op jit(solution)/shard_map/all_to_all | solution.py:18
  101.0 9.7 %reshape.53 = f32[8192,2,64]{2,1,0:T(2,128)} reshape(f32[16,65536]{1,0:T(8,128)} %reduce.8) | data formatting | bytes 8388608
  110.7 12.2 %copy.26 = f32[2,64,16,512]{3,1,2,0:T(8,128)} copy(f32[2,64,16,512]{1,0,3,2:T(2,128)} %bitcast.96) | data formatting | bytes 8388608 | tf_op jit(solution)/shard_map/all_to_all | solution.py:18
  122.9 17.6 %convolution_bitcast_fusion = f32[1024,1024]{1,0:T(8,128)} fusion(f32[2,1024,512]{2,1,0:T(8,128)} %bitcast.98), kind=kOutput, calls=%fused_computation.4 | convolution fusion | flops 12884901888 | bytes 8388608 | tf_op jit(solution)/shard_map/crm,csm->rs/dot_general | solution.py:20
  140.6 270.4 %all-reduce.3.cloned.1.call-done = f32[1024,1024]{1,0:T(8,128)} async-done(((f32[1024,1024]{1,0:T(8,128)}), f32[1024,1024]{1,0:T(8,128)}) %all-reduce.3.cloned.1.call-update) | async-done | bytes 4194320 | tf_op jit(solution)/shard_map/psum | solution.py:21
  411.0 5.5 fusion.32
  416.5 1.8 fusion.33
  418.5 11.7 %cholesky.130 = f32[128,128]{1,0:T(8,128)S(1)} custom-call(f32[128,128]{1,0:T(8,128)S(1)} %cholesky.194), custom_call_target="Cholesky" | custom-call | tf_op jit(solution)/shard_map/jit(cholesky)/cholesky | solution.py:11
  430.3 9.8 %custom-call.13 = f32[1,128,128]{1,2,0:T(8,128)S(1)} custom-call(f32[1,128,128]{2,1,0:T(8,128)S(1)} %get-tuple-element.53), custom_call_target="InvertDiagBlocksLowerTriangular" | custom-call | tf_op jit(solution)/shard_map/jit(cholesky)/cholesky | solution.py:11
  440.6 11.7 %cholesky.147 = f32[128,128]{1,0:T(8,128)S(1)} custom-call(f32[128,128]{1,0:T(8,128)S(1)} %convolution_subtract_fusion.3), custom_call_target="Cholesky" | custom-call | tf_op jit(solution)/shard_map/jit(cholesky)/cholesky | solution.py:11
  467.2 3.9 while.4
  467.8 1.4 bitcast_dynamic-update-slice_fusion.4
  469.8 1.4 bitcast_dynamic-update-slice_fusion.4
  471.2 19.7 %custom-call.14 = f32[2,128,128]{1,2,0:T(8,128)S(1)} custom-call(f32[2,128,128]{2,1,0:T(8,128)S(1)} %get-tuple-element.18), custom_call_target="InvertDiagBlocksLowerTriangular" | custom-call | tf_op jit(solution)/shard_map/jit(_solve_triangular)/triangular_solve | solution.py:12
  493.2 5.3 fusion.2
  498.5 1.8 fusion.34
  500.5 11.7 %cholesky.164 = f32[128,128]{1,0:T(8,128)S(1)} custom-call(f32[128,128]{1,0:T(8,128)S(1)} %cholesky.197), custom_call_target="Cholesky" | custom-call | tf_op jit(solution)/shard_map/jit(cholesky)/cholesky | solution.py:11
  512.3 9.8 %custom-call.15 = f32[1,128,128]{1,2,0:T(8,128)S(1)} custom-call(f32[1,128,128]{2,1,0:T(8,128)S(1)} %get-tuple-element.49), custom_call_target="InvertDiagBlocksLowerTriangular" | custom-call | tf_op jit(solution)/shard_map/jit(cholesky)/cholesky | solution.py:11
  522.6 11.7 %cholesky.181 = f32[128,128]{1,0:T(8,128)S(1)} custom-call(f32[128,128]{1,0:T(8,128)S(1)} %convolution_subtract_fusion.2), custom_call_target="Cholesky" | custom-call | tf_op jit(solution)/shard_map/jit(cholesky)/cholesky | solution.py:11
  537.2 4.0 while.5
  537.8 1.4 bitcast_dynamic-update-slice_fusion.5
  539.8 1.4 bitcast_dynamic-update-slice_fusion.5
  541.2 19.7 %custom-call.16 = f32[2,128,128]{1,2,0:T(8,128)S(1)} custom-call(f32[2,128,128]{2,1,0:T(8,128)S(1)} %get-tuple-element.19), custom_call_target="InvertDiagBlocksLowerTriangular" | custom-call | tf_op jit(solution)/shard_map/jit(_solve_triangular)/triangular_solve | solution.py:12
  563.2 5.7 convolution_bitcast_fusion.1
  568.9 1.8 copy.20
  570.7 4.6 all-to-all-start.1
  576.1 17.8 %all-to-all-done.1 = f32[2,256,512]{2,0,1:T(2,128)} async-done(((f32[2,256,512]{2,0,1:T(2,128)}), f32[2,256,512]{2,0,1:T(2,128)}, u32[]{:S(2)}, u32[]{:S(2)}) %all-to-all-start.1) | async-done | bytes 1048608 | tf_op jit(solution)/shard_map/all_to_all | solution.py:26
  593.9 1.8 copy.21
  595.7 1.0 reshape.27
  (46 shorter events, 12.1 us)
Async XLA Ops:
  7.2 403.9 %copy-start = (f32[1024,256]{1,0:T(8,128)S(1)}, f32[1024,256]{1,0:T(8,128)}, u32[]{:S(2)}) copy-start(f32[1024,256]{1,0:T(8,128)} %param.6) | copy-start | bytes 3145732
  7.2 403.8 %all-reduce.3.cloned.1.call-start = ((), (), s32[]{:S(2)}) async-start(), calls=%async_computation.2 | async-start | bytes 8388608 | tf_op jit(solution)/shard_map/psum | solution.py:21
  570.7 23.2 %all-to-all-start.1 = ((f32[2,256,512]{2,0,1:T(2,128)}), f32[2,256,512]{2,0,1:T(2,128)}, u32[]{:S(2)}, u32[]{:S(2)}) async-start(f32[2,256,512]{2,0,1:T(2,128)} %copy.20), calls=%async_computation.1 | async-start | bytes 2097152 | tf_op jit(solution)/shard_map/all_to_all | solution.py:26
Sparse Core Ops, SparseCore 0:
  140.7 270.2 all-reduce.2
where the time goes:
time: 614 us; the launch traced here: 604 us
  waiting for transfers between devices  288 us (47%)
  other arithmetic  122 us (20%)
  local copies, waits for them, and re-layouts  59.5 us (10%)
  blocking collectives  56.1 us (9%)
  matrix products  43.3 us (7%)
  between operations  30.1 us (5%)
    psum x1, waiting for transfers between devices, per_device(): gram = lax.psum(local_gram, ('gx', 'gy', 'gz'))  270 us
    another operation x13, other arithmetic, orthonormal(): lower = jnp.linalg.cholesky(small)  68.5 us
    all_to_all x1, blocking collectives, per_device(): lax.all_to_all(flat_field, 'gx', split_axis=2, concat_axis=1, tiled=True)  56.1 us
    another operation x5, other arithmetic, orthonormal(): return jax.scipy.linalg.solve_triangular(lower, image.T, lower=True).T  39.6 us
    unnamed x6, local copies, waits for them, and re-layouts  33.9 us
    all_to_all x1, waiting for transfers between devices, per_device(): lax.all_to_all(projected, 'gx', split_axis=1, concat_axis=2, tiled=True)  17.8 us
    dot_general x1, matrix products, per_device(): jnp.einsum('crm,csm->rs', fibers, fibers, precision=lax.Precision.HIGHEST)  17.6 us
    all_to_all x1, other arithmetic, per_device(): lax.all_to_all(flat_field, 'gx', split_axis=2, concat_axis=1, tiled=True)  13.7 us
  transfers between devices with their start and end apart: 2, of which 2 were waited for; matrix products, arithmetic and copies ran while one was open for 0% of the time, Pallas kernels for 0%

commit v1 on v0

--- a/solution.py
+++ b/solution.py
@@ -4,6 +4,17 @@
 from jax.sharding import PartitionSpec as P
 
 ITERS = 2
+
+
+def split_up(value, dim, peers):
+    before, after = (value.shape[:dim], value.shape[dim + 1 :])
+    return jnp.moveaxis(value.reshape(*before, peers, -1, *after), dim, 0)
+
+
+def laid_out(blocks, dim):
+    blocks = jnp.moveaxis(blocks, 0, dim)
+    shape = blocks.shape
+    return blocks.reshape(*shape[:dim], shape[dim] * shape[dim + 1], *shape[dim + 2 :])
 
 
 def orthonormal(image):
@@ -23,7 +34,14 @@
         image = jnp.dot(gram, basis, precision=lax.Precision.HIGHEST)
         basis = orthonormal(image)
     projected = jnp.einsum("rk,crm->ckm", basis, fibers, precision=lax.Precision.HIGHEST)
-    returned = lax.all_to_all(projected, "gx", split_axis=1, concat_axis=2, tiled=True)
+    size, index = (lax.axis_size("gx"), lax.axis_index("gx"))
+    blocks = split_up(projected, 1, size)
+    finished = [blocks[index]]
+    for k in range(1, size):
+        sent = blocks[index ^ k]
+        finished.append(lax.ppermute(sent, "gx", [(i, i ^ k) for i in range(size)]))
+    blocks = jnp.stack(finished)[index ^ jnp.arange(size)]
+    returned = laid_out(blocks, 2)
     offset = lax.axis_index("gx") * slab
     factor = lax.dynamic_slice_in_dim(basis, offset, slab, 0)
     return (factor, returned.reshape(comps, returned.shape[1], cells_y, cells_z))

time: 614 us -> 633 us (1.031)
  the two profiles are of different devices: /device:TPU:97 before, /device:TPU:6 now
where the time goes in v1:
time: 633 us; the launch traced here: 622 us
  waiting for transfers between devices  275 us (43%)
  other arithmetic  122 us (19%)
  local copies, waits for them, and re-layouts  62.4 us (10%)
  blocking collectives  56.9 us (9%)
  matrix products  43.3 us (7%)
  starting transfers between devices  32.4 us (5%)
  between operations  30.4 us (5%)
    psum x1, waiting for transfers between devices, per_device(): gram = lax.psum(local_gram, ('gx', 'gy', 'gz'))  270 us
    another operation x13, other arithmetic, orthonormal(): lower = jnp.linalg.cholesky(small)  68.6 us
    all_to_all x1, blocking collectives, per_device(): lax.all_to_all(flat_field, 'gx', split_axis=2, concat_axis=1, tiled=True)  56.9 us
    another operation x5, other arithmetic, orthonormal(): return jax.scipy.linalg.solve_triangular(lower, image.T, lower=True).T  39.6 us
    unnamed x21, local copies, waits for them, and re-layouts  38.2 us
    ppermute x15, starting transfers between devices, per_device(): finished.append(lax.ppermute(sent, 'gx', [(i, i ^ k) for i in range(size)]))  32.4 us
    dot_general x1, matrix products, per_device(): jnp.einsum('crm,csm->rs', fibers, fibers, precision=lax.Precision.HIGHEST)  17.6 us
    all_to_all x1, other arithmetic, per_device(): lax.all_to_all(flat_field, 'gx', split_axis=2, concat_axis=1, tiled=True)  13.7 us
  transfers between devices with their start and end apart: 16, of which 2 were waited for; matrix products, arithmetic and copies ran while one was open for 1% of the time, Pallas kernels for 0%

profile of v1, /device:TPU:6, one launch (start us, length us, event | category | flops | bytes accessed | tf_op | source)
XLA Modules:
  0.0 622.3 jit_solution(9169383479604928725)
XLA Ops:
  7.2 8.4 %copy.18 = f32[2,64,64,128]{1,0,3,2:T(2,128)} copy(f32[2,64,64,128]{3,2,1,0:T(8,128)} %param.5) | data formatting | bytes 8388608 | tf_op args[0]
  15.7 15.1 %reshape.106 = f32[16,1,65536]{2,1,0:T(1,128)} reshape(f32[8192,2,64]{2,1,0:T(2,128)} %bitcast.160) | data formatting | bytes 8388608
  30.8 56.9 %all_to_all.18 = f32[16,1,65536]{2,1,0:T(1,128)} all-to-all(f32[16,1,65536]{2,1,0:T(1,128)} %reshape.106), channel_id=1, replica_groups=mesh['gx'=16,'gy'=2,'gz'=8] {'gx'}, dimensions={0} | all-to-all | bytes 8388608 | tf_op jit(solution)/shard_map/all_to_all | solution.py:29
  88.2 13.7 %reduce.8 = f32[16,65536]{1,0:T(8,128)} reduce(f32[16,1,65536]{2,1,0:T(1,128)} %all_to_all.18, f32[]{:T(128)} %broadcast.122), dimensions={1}, to_apply=%all_to_all.13.reduce_sub_computation | reduce | bytes 8388612 | tf_op jit(solution)/shard_map/all_to_all | solution.py:29
  101.9 9.7 %reshape.107 = f32[8192,2,64]{2,1,0:T(2,128)} reshape(f32[16,65536]{1,0:T(8,128)} %reduce.8) | data formatting | bytes 8388608
  111.5 12.2 %copy.30 = f32[2,64,16,512]{3,1,2,0:T(8,128)} copy(f32[2,64,16,512]{1,0,3,2:T(2,128)} %bitcast.159) | data formatting | bytes 8388608 | tf_op jit(solution)/shard_map/all_to_all | solution.py:29
  123.7 17.6 %convolution_bitcast_fusion = f32[1024,1024]{1,0:T(8,128)} fusion(f32[2,1024,512]{2,1,0:T(8,128)} %bitcast.161), kind=kOutput, calls=%fused_computation.5 | convolution fusion | flops 12884901888 | bytes 8388608 | tf_op jit(solution)/shard_map/crm,csm->rs/dot_general | solution.py:31
  141.5 269.7 %all-reduce.3.cloned.1.call-done = f32[1024,1024]{1,0:T(8,128)} async-done(((f32[1024,1024]{1,0:T(8,128)}), f32[1024,1024]{1,0:T(8,128)}) %all-reduce.3.cloned.1.call-update) | async-done | bytes 4194320 | tf_op jit(solution)/shard_map/psum | solution.py:32
  411.3 5.5 fusion.34
  416.7 1.8 fusion.35
  418.8 11.7 %cholesky.130 = f32[128,128]{1,0:T(8,128)S(1)} custom-call(f32[128,128]{1,0:T(8,128)S(1)} %cholesky.194), custom_call_target="Cholesky" | custom-call | tf_op jit(solution)/shard_map/jit(cholesky)/cholesky | solution.py:22
  430.5 9.8 %custom-call.13 = f32[1,128,128]{1,2,0:T(8,128)S(1)} custom-call(f32[1,128,128]{2,1,0:T(8,128)S(1)} %get-tuple-element.70), custom_call_target="InvertDiagBlocksLowerTriangular" | custom-call | tf_op jit(solution)/shard_map/jit(cholesky)/cholesky | solution.py:22
  440.8 11.7 %cholesky.147 = f32[128,128]{1,0:T(8,128)S(1)} custom-call(f32[128,128]{1,0:T(8,128)S(1)} %convolution_subtract_fusion.3), custom_call_target="Cholesky" | custom-call | tf_op jit(solution)/shard_map/jit(cholesky)/cholesky | solution.py:22
  467.6 4.1 while.4
  471.7 19.7 %custom-call.14 = f32[2,128,128]{1,2,0:T(8,128)S(1)} custom-call(f32[2,128,128]{2,1,0:T(8,128)S(1)} %get-tuple-element.18), custom_call_target="InvertDiagBlocksLowerTriangular" | custom-call | tf_op jit(solution)/shard_map/jit(_solve_triangular)/triangular_solve | solution.py:23
  493.7 5.3 fusion.3
  499.0 1.8 fusion.36
  501.1 11.7 %cholesky.164 = f32[128,128]{1,0:T(8,128)S(1)} custom-call(f32[128,128]{1,0:T(8,128)S(1)} %cholesky.197), custom_call_target="Cholesky" | custom-call | tf_op jit(solution)/shard_map/jit(cholesky)/cholesky | solution.py:22
  512.9 9.8 %custom-call.15 = f32[1,128,128]{1,2,0:T(8,128)S(1)} custom-call(f32[1,128,128]{2,1,0:T(8,128)S(1)} %get-tuple-element.66), custom_call_target="InvertDiagBlocksLowerTriangular" | custom-call | tf_op jit(solution)/shard_map/jit(cholesky)/cholesky | solution.py:22
  523.2 11.7 %cholesky.181 = f32[128,128]{1,0:T(8,128)S(1)} custom-call(f32[128,128]{1,0:T(8,128)S(1)} %convolution_subtract_fusion.2), custom_call_target="Cholesky" | custom-call | tf_op jit(solution)/shard_map/jit(cholesky)/cholesky | solution.py:22
  537.7 4.0 while.5
  541.8 19.7 %custom-call.16 = f32[2,128,128]{1,2,0:T(8,128)S(1)} custom-call(f32[2,128,128]{2,1,0:T(8,128)S(1)} %get-tuple-element.19), custom_call_target="InvertDiagBlocksLowerTriangular" | custom-call | tf_op jit(solution)/shard_map/jit(_solve_triangular)/triangular_solve | solution.py:23
  563.7 5.7 fusion.1
  571.5 1.8 collective-permute-start.1
  573.3 1.7 collective-permute-start.2
  577.3 4.2 collective-permute-start.5
  582.3 1.6 collective-permute-start.6
  588.3 6.4 %collective-permute-start.9 = (f32[2,16,512]{2,1,0:T(8,128)S(1)}, f32[2,16,512]{2,1,0:T(8,128)S(1)}, u32[]{:S(2)}, u32[]{:S(2)}) collective-permute-start(f32[2,16,512]{2,1,0:T(8,128)S(1)} %get-tuple-element.53), channel_id=1, source_target_pairs={{0,160},{16,176},{32,128},{48,144},{64,224},{80,240},{96,192},{112... | collective-permute-start | bytes 196616 | tf_op jit(solution)/shard_map/ppermute | solution.py:42
  595.6 2.4 collective-permute-start.10
  598.7 6.4 %collective-permute-start.13 = (f32[2,16,512]{2,1,0:T(8,128)S(1)}, f32[2,16,512]{2,1,0:T(8,128)S(1)}, u32[]{:S(2)}, u32[]{:S(2)}) collective-permute-start(f32[2,16,512]{2,1,0:T(8,128)S(1)} %get-tuple-element.49), channel_id=1, source_target_pairs={{0,224},{16,240},{32,192},{48,208},{64,160},{80,176},{96,128},{112... | collective-permute-start | bytes 196616 | tf_op jit(solution)/shard_map/ppermute | solution.py:42
  605.1 2.8 collective-permute-start.14
  608.0 4.8 collective-permute-done.14
  (93 shorter events, 30.3 us)
Async XLA Ops:
  7.2 404.1 %copy-start = (f32[1024,256]{1,0:T(8,128)S(1)}, f32[1024,256]{1,0:T(8,128)}, u32[]{:S(2)}) copy-start(f32[1024,256]{1,0:T(8,128)} %param.6) | copy-start | bytes 3145732
  7.2 404.1 %all-reduce.3.cloned.1.call-start = ((), (), s32[]{:S(2)}) async-start(), calls=%async_computation.1 | async-start | bytes 8388608 | tf_op jit(solution)/shard_map/psum | solution.py:32
  570.3 6.9 %collective-permute-start = (f32[2,16,512]{2,1,0:T(8,128)}, f32[2,16,512]{2,1,0:T(8,128)}, u32[]{:S(2)}, u32[]{:S(2)}) collective-permute-start(f32[2,16,512]{2,1,0:T(8,128)} %get-tuple-element.62), channel_id=1, source_target_pairs={{0,16},{16,0},{32,48},{48,32},{64,80},{80,64},{96,112},{112,96},{1... | collective-permute-start | bytes 196616 | tf_op jit(solution)/shard_map/ppermute | solution.py:42
  571.5 10.9 %collective-permute-start.1 = (f32[2,16,512]{2,1,0:T(8,128)}, f32[2,16,512]{2,1,0:T(8,128)}, u32[]{:S(2)}, u32[]{:S(2)}) collective-permute-start(f32[2,16,512]{2,1,0:T(8,128)} %get-tuple-element.61), channel_id=1, source_target_pairs={{0,32},{16,48},{32,0},{48,16},{64,96},{80,112},{96,64},{112,80},{1... | collective-permute-start | bytes 196616 | tf_op jit(solution)/shard_map/ppermute | solution.py:42
  573.3 11.5 %collective-permute-start.2 = (f32[2,16,512]{2,1,0:T(8,128)}, f32[2,16,512]{2,1,0:T(8,128)}, u32[]{:S(2)}, u32[]{:S(2)}) collective-permute-start(f32[2,16,512]{2,1,0:T(8,128)} %get-tuple-element.60), channel_id=1, source_target_pairs={{0,48},{16,32},{32,16},{48,0},{64,112},{80,96},{96,80},{112,64},{1... | collective-permute-start | bytes 196616 | tf_op jit(solution)/shard_map/ppermute | solution.py:42
  575.0 12.1 %collective-permute-start.3 = (f32[2,16,512]{2,1,0:T(8,128)}, f32[2,16,512]{2,1,0:T(8,128)}, u32[]{:S(2)}, u32[]{:S(2)}) collective-permute-start(f32[2,16,512]{2,1,0:T(8,128)} %get-tuple-element.59), channel_id=1, source_target_pairs={{0,64},{16,80},{32,96},{48,112},{64,0},{80,16},{96,32},{112,48},{1... | collective-permute-start | bytes 196616 | tf_op jit(solution)/shard_map/ppermute | solution.py:42
  575.9 12.5 %collective-permute-start.4 = (f32[2,16,512]{2,1,0:T(8,128)}, f32[2,16,512]{2,1,0:T(8,128)}, u32[]{:S(2)}, u32[]{:S(2)}) collective-permute-start(f32[2,16,512]{2,1,0:T(8,128)} %get-tuple-element.58), channel_id=1, source_target_pairs={{0,80},{16,64},{32,112},{48,96},{64,16},{80,0},{96,48},{112,32},{1... | collective-permute-start | bytes 196616 | tf_op jit(solution)/shard_map/ppermute | solution.py:42
  577.3 18.3 %collective-permute-start.5 = (f32[2,16,512]{2,1,0:T(8,128)}, f32[2,16,512]{2,1,0:T(8,128)S(1)}, u32[]{:S(2)}, u32[]{:S(2)}) collective-permute-start(f32[2,16,512]{2,1,0:T(8,128)} %get-tuple-element.57), channel_id=1, source_target_pairs={{0,96},{16,112},{32,64},{48,80},{64,32},{80,48},{96,0},{112,16},{1... | collective-permute-start | bytes 196616 | tf_op jit(solution)/shard_map/ppermute | solution.py:42
  582.3 15.7 %collective-permute-start.6 = (f32[2,16,512]{2,1,0:T(8,128)}, f32[2,16,512]{2,1,0:T(8,128)S(1)}, u32[]{:S(2)}, u32[]{:S(2)}) collective-permute-start(f32[2,16,512]{2,1,0:T(8,128)} %get-tuple-element.56), channel_id=1, source_target_pairs={{0,112},{16,96},{32,80},{48,64},{64,48},{80,32},{96,16},{112,0},{1... | collective-permute-start | bytes 196616 | tf_op jit(solution)/shard_map/ppermute | solution.py:42
  584.8 13.7 %collective-permute-start.7 = (f32[2,16,512]{2,1,0:T(8,128)}, f32[2,16,512]{2,1,0:T(8,128)S(1)}, u32[]{:S(2)}, u32[]{:S(2)}) collective-permute-start(f32[2,16,512]{2,1,0:T(8,128)} %get-tuple-element.55), channel_id=1, source_target_pairs={{0,128},{16,144},{32,160},{48,176},{64,192},{80,208},{96,224},{112... | collective-permute-start | bytes 196616 | tf_op jit(solution)/shard_map/ppermute | solution.py:42
  587.2 11.5 %collective-permute-start.8 = (f32[2,16,512]{2,1,0:T(8,128)}, f32[2,16,512]{2,1,0:T(8,128)S(1)}, u32[]{:S(2)}, u32[]{:S(2)}) collective-permute-start(f32[2,16,512]{2,1,0:T(8,128)} %get-tuple-element.54), channel_id=1, source_target_pairs={{0,144},{16,128},{32,176},{48,160},{64,208},{80,192},{96,240},{112... | collective-permute-start | bytes 196616 | tf_op jit(solution)/shard_map/ppermute | solution.py:42
  588.3 16.7 %collective-permute-start.9 = (f32[2,16,512]{2,1,0:T(8,128)S(1)}, f32[2,16,512]{2,1,0:T(8,128)S(1)}, u32[]{:S(2)}, u32[]{:S(2)}) collective-permute-start(f32[2,16,512]{2,1,0:T(8,128)S(1)} %get-tuple-element.53), channel_id=1, source_target_pairs={{0,160},{16,176},{32,128},{48,144},{64,224},{80,240},{96,192},{112... | collective-permute-start | bytes 196616 | tf_op jit(solution)/shard_map/ppermute | solution.py:42
  595.6 12.3 %collective-permute-start.10 = (f32[2,16,512]{2,1,0:T(8,128)S(1)}, f32[2,16,512]{2,1,0:T(8,128)S(1)}, u32[]{:S(2)}, u32[]{:S(2)}) collective-permute-start(f32[2,16,512]{2,1,0:T(8,128)S(1)} %get-tuple-element.52), channel_id=1, source_target_pairs={{0,176},{16,160},{32,144},{48,128},{64,240},{80,224},{96,208},{112... | collective-permute-start | bytes 196616 | tf_op jit(solution)/shard_map/ppermute | solution.py:42
  598.0 9.9 %collective-permute-start.11 = (f32[2,16,512]{2,1,0:T(8,128)S(1)}, f32[2,16,512]{2,1,0:T(8,128)S(1)}, u32[]{:S(2)}, u32[]{:S(2)}) collective-permute-start(f32[2,16,512]{2,1,0:T(8,128)S(1)} %get-tuple-element.51), channel_id=1, source_target_pairs={{0,192},{16,208},{32,224},{48,240},{64,128},{80,144},{96,160},{112... | collective-permute-start | bytes 196616 | tf_op jit(solution)/shard_map/ppermute | solution.py:42
  598.5 9.4 %collective-permute-start.12 = (f32[2,16,512]{2,1,0:T(8,128)S(1)}, f32[2,16,512]{2,1,0:T(8,128)S(1)}, u32[]{:S(2)}, u32[]{:S(2)}) collective-permute-start(f32[2,16,512]{2,1,0:T(8,128)S(1)} %get-tuple-element.50), channel_id=1, source_target_pairs={{0,208},{16,192},{32,240},{48,224},{64,144},{80,128},{96,176},{112... | collective-permute-start | bytes 196616 | tf_op jit(solution)/shard_map/ppermute | solution.py:42
  598.7 9.3 %collective-permute-start.13 = (f32[2,16,512]{2,1,0:T(8,128)S(1)}, f32[2,16,512]{2,1,0:T(8,128)S(1)}, u32[]{:S(2)}, u32[]{:S(2)}) collective-permute-start(f32[2,16,512]{2,1,0:T(8,128)S(1)} %get-tuple-element.49), channel_id=1, source_target_pairs={{0,224},{16,240},{32,192},{48,208},{64,160},{80,176},{96,128},{112... | collective-permute-start | bytes 196616 | tf_op jit(solution)/shard_map/ppermute | solution.py:42
  605.1 7.7 %collective-permute-start.14 = (f32[2,16,512]{2,1,0:T(8,128)S(1)}, f32[2,16,512]{2,1,0:T(8,128)S(1)}, u32[]{:S(2)}, u32[]{:S(2)}) collective-permute-start(f32[2,16,512]{2,1,0:T(8,128)S(1)} %get-tuple-element.48), channel_id=1, source_target_pairs={{0,240},{16,224},{32,208},{48,192},{64,176},{80,160},{96,144},{112... | collective-permute-start | bytes 196616 | tf_op jit(solution)/shard_map/ppermute | solution.py:42
Sparse Core Ops, SparseCore 0:
  141.5 269.6 all-reduce.2
